TPU v7x, 256 devices: a whole 4x4x8 slice. The times are simulated.
256 devices in a mesh: seq: 32 (over x, z_hi, core), tp: 8 (over z_lo, y).
Axes of the slice: x: 4, y: 4, z: 8 (z_hi: 4, z_lo: 2; z = z_hi * 2 + z_lo), core: 2. Of those that a mesh axis runs over, the one named last changes fastest.
Arguments:
- tokens: bfloat16 [1024, 8192], P('tp', 'seq'), may hold values from -6 to 6
- gate_weight: bfloat16 [8192, 14336], P('seq', 'tp'), may hold values from -0.0625 to 0.0625
- up_weight: bfloat16 [8192, 14336], P('seq', 'tp'), may hold values from -0.0625 to 0.0625
- down_weight: bfloat16 [14336, 8192], P('tp', 'seq'), may hold values from -0.09375 to 0.09375
- masks: int32 [8, 112], P(None, 'tp'), may hold values from 0 to 1, as said below
- cotangent: bfloat16 [1024, 8192], P('tp', 'seq'), may hold values from -6 to 6
Outputs:
- output: bfloat16 [1024, 8192], P('tp', 'seq')
- grad_tokens: bfloat16 [1024, 8192], P('tp', 'seq')
- grad_gate: float32 [8192, 14336], P('seq', 'tp')
- grad_up: float32 [8192, 14336], P('seq', 'tp')
- grad_down: float32 [14336, 8192], P('tp', 'seq')
Inputs may be any that keep to these rules, and one draw needn't show every extreme that they name: Each row of masks holds exactly 28 ones. Cut a row into 8 groups of 14 consecutive blocks: in every row one group holds exactly 7 ones, and the remaining ones are spread over the other groups as evenly as possible, so that their counts differ by at most one.
All inputs are finite; a program needn't handle non-finite values.
Results may differ from a plain program's by a relative error of at most 0.0049.
Values may be sent and summed in bfloat16 or wider, within the bound.
No kernel may reach another device: no remote copies, remote signals or barrier semaphores. Data moves between devices by JAX's collectives and lax.ppermute only.
A program may use at most 128 MiB of HBM per device.

v0:
```python
import math

import jax
import jax.numpy as jnp
from jax import lax
from jax.sharding import PartitionSpec as P

FF = 14336
BLK = 128
ROWBLK = 128


def sent_together(arrays, axis, dim, along):
    ends, at = ([], 0)
    for a in arrays[:-1]:
        at += a.shape[along]
        ends.append(at)
    both = jnp.concatenate(arrays, axis=along)
    return tuple(
        jnp.split(lax.psum_scatter(both, axis, scatter_dimension=dim, tiled=True), ends, axis=along)
    )


def copy_for_each(array, axis):
    devices = lax.axis_size(axis)
    return lax.all_to_all(
        jnp.broadcast_to(array[None], (devices, *array.shape)), axis, 0, 0, tiled=True
    )


def laid_out(tiles, dim):
    lengths = list(tiles.shape[1:])
    lengths[dim] *= tiles.shape[0]
    return jnp.moveaxis(tiles, 0, dim).reshape(lengths)


def gathered_copies(array, axis, dim):
    tiles = copy_for_each(array, axis)
    return laid_out(tiles, dim)


def cut_along(array, dim, devices):
    lengths = array.shape
    tiles = array.reshape(*lengths[:dim], devices, lengths[dim] // devices, *lengths[dim + 1 :])
    return jnp.moveaxis(tiles, dim, 0)


def sum_at_owner(array, axis, dim):
    tiles = cut_along(array, dim, lax.axis_size(axis))
    arrived = lax.all_to_all(tiles, axis, split_axis=0, concat_axis=0, tiled=True)
    return arrived.sum(axis=0)


def sent_together_2(arrays, axis, dim, along):
    widths = [a.shape[along] for a in arrays]
    both = jnp.concatenate(arrays, axis=along)
    filled = lax.all_gather(both, axis, axis=dim, tiled=True)
    return tuple(jnp.split(filled, [sum(widths[:k]) for k in range(1, len(widths))], axis=along))


def slot_tables(mask_local, capacity):
    running_total = jnp.cumsum(mask_local, axis=1) - 1
    slot_ids = jnp.arange(capacity, dtype=jnp.int32)
    block_ids = jnp.arange(mask_local.shape[1], dtype=jnp.int32)
    slot_hit = (mask_local[:, None, :] == 1) & (
        running_total[:, None, :] == slot_ids[None, :, None]
    )
    slot_indicator = slot_hit.astype(jnp.float32)
    slot_block = jnp.sum(jnp.where(slot_hit, block_ids[None, None, :], 0), axis=2)
    slot_live = jnp.sum(slot_indicator, axis=2)
    return (slot_indicator, slot_block, slot_live)


def rows_live(slot_live, row_start, row_count):
    row_block = (row_start + jnp.arange(row_count, dtype=jnp.int32)) // ROWBLK
    select = (
        row_block[:, None] == jnp.arange(slot_live.shape[0], dtype=jnp.int32)[None, :]
    ).astype(jnp.float32)
    live = jnp.dot(select, slot_live, preferred_element_type=jnp.float32)
    return jnp.repeat(live, BLK, axis=1)


def shards(tokens, gate_weight, up_weight, down_weight, masks, cotangent):
    seq_count = lax.axis_size("seq")
    tp_count = lax.axis_size("tp")
    all_rows, grad_rows = (
        lax.all_gather(tokens, "tp", axis=0, tiled=True),
        lax.all_gather(cotangent, "tp", axis=0, tiled=True),
    )
    total_row_count = all_rows.shape[0]
    feat_cols = all_rows.shape[1]
    local_blocks = masks.shape[1]
    row_blocks = total_row_count // ROWBLK
    kept_total = FF // BLK // 4
    capacity = 2 * kept_total // tp_count
    packed_cols = capacity * BLK
    slot_indicator, slot_block, slot_live = slot_tables(masks, capacity)
    gate_blocks = jnp.take(gate_weight.reshape(feat_cols, local_blocks, BLK), slot_block, axis=1)
    up_blocks = jnp.take(up_weight.reshape(feat_cols, local_blocks, BLK), slot_block, axis=1)
    down_blocks = jnp.take(down_weight.reshape(local_blocks, BLK, feat_cols), slot_block, axis=0)
    token_blocks = all_rows.reshape(row_blocks, ROWBLK, feat_cols)
    gate_part = jnp.einsum(
        "rtd,drck->rtck", token_blocks, gate_blocks, preferred_element_type=jnp.float32
    ).reshape(total_row_count, packed_cols)
    up_part = jnp.einsum(
        "rtd,drck->rtck", token_blocks, up_blocks, preferred_element_type=jnp.float32
    ).reshape(total_row_count, packed_cols)
    own_rows = total_row_count // seq_count
    own_start = lax.axis_index("seq") * own_rows
    local_live_blocks = rows_live(slot_live, own_start, own_rows)
    gate_own, up_own = sent_together((gate_part, up_part), "seq", 0, 1)
    hidden_own = (jax.nn.silu(gate_own) * up_own * local_live_blocks).astype(jnp.bfloat16)
    hidden = gathered_copies(hidden_own, "seq", 0)
    hidden_blocks = hidden.reshape(row_blocks, ROWBLK, capacity, BLK)
    output_part = jnp.einsum(
        "rtck,rckd->rtd", hidden_blocks, down_blocks, preferred_element_type=jnp.float32
    ).reshape(total_row_count, feat_cols)
    output = sum_at_owner(output_part, "tp", 0).astype(jnp.bfloat16)
    grad_blocks = grad_rows.reshape(row_blocks, ROWBLK, feat_cols)
    hidden_part = jnp.einsum(
        "rtd,rckd->rtck", grad_blocks, down_blocks, preferred_element_type=jnp.float32
    ).reshape(total_row_count, packed_cols)
    grad_hidden = (
        lax.psum_scatter(hidden_part, "seq", scatter_dimension=0, tiled=True) * local_live_blocks
    )
    sigmoid_gate = jax.nn.sigmoid(gate_own)
    grad_gate_own = (
        grad_hidden * up_own * sigmoid_gate * (1.0 + gate_own * (1.0 - sigmoid_gate))
    ).astype(jnp.bfloat16)
    grad_up_own = (grad_hidden * gate_own * sigmoid_gate).astype(jnp.bfloat16)
    grad_gate_act, grad_up_act = sent_together_2((grad_gate_own, grad_up_own), "seq", 0, 1)
    grad_scale = 1.0 / math.sqrt(total_row_count)
    gate_act_blocks = grad_gate_act.reshape(row_blocks, ROWBLK, capacity, BLK)
    up_act_blocks = grad_up_act.reshape(row_blocks, ROWBLK, capacity, BLK)
    down_compact = jnp.einsum(
        "rtck,rtd->rckd", hidden_blocks, grad_blocks, preferred_element_type=jnp.float32
    )
    grad_down = jnp.einsum(
        "toh,toye->hye", slot_indicator, down_compact, precision=lax.Precision.HIGHEST
    )
    grad_down = grad_down.reshape(local_blocks * BLK, feat_cols) * grad_scale
    gate_packed = jnp.einsum(
        "rtd,rtck->drck", token_blocks, gate_act_blocks, preferred_element_type=jnp.float32
    )
    grad_gate = jnp.einsum(
        "rcb,drck->dbk", slot_indicator, gate_packed, precision=lax.Precision.HIGHEST
    )
    grad_gate = grad_gate.reshape(feat_cols, local_blocks * BLK) * grad_scale
    up_packed = jnp.einsum(
        "rtd,rtck->drck", token_blocks, up_act_blocks, preferred_element_type=jnp.float32
    )
    grad_up = jnp.einsum(
        "rcb,drck->dbk", slot_indicator, up_packed, precision=lax.Precision.HIGHEST
    )
    grad_up = grad_up.reshape(feat_cols, local_blocks * BLK) * grad_scale
    input_part = jnp.einsum(
        "rtck,drck->rtd", gate_act_blocks, gate_blocks, preferred_element_type=jnp.float32
    ) + jnp.einsum("rtck,drck->rtd", up_act_blocks, up_blocks, preferred_element_type=jnp.float32)
    input_part = input_part.reshape(total_row_count, feat_cols)
    grad_tokens = sum_at_owner(input_part, "tp", 0).astype(jnp.bfloat16)
    return (output, grad_tokens, grad_gate, grad_up, grad_down)


def solution(mesh):
    placed = (
        P("tp", "seq"),
        P("seq", "tp"),
        P("seq", "tp"),
        P("tp", "seq"),
        P(None, "tp"),
        P("tp", "seq"),
    )
    return jax.shard_map(
        shards,
        mesh=mesh,
        in_specs=placed,
        out_specs=(P("tp", "seq"), P("tp", "seq"), P("seq", "tp"), P("seq", "tp"), P("tp", "seq")),
        check_vma=False,
    )
```

profile of v0, /device:TPU:1, one launch (start us, length us, event | category | flops | bytes accessed | tf_op | source)
XLA Modules:
  0.0 453.4 jit_solution(619394102101486757)
XLA Ops:
  7.2 0.8 broadcast_compare_fusion
  8.0 0.8 reduce_window_sum.11
  8.8 0.2 select_reduce_fusion
  9.1 0.1 copy.53
  9.2 0.1 copy.37
  9.3 25.0 %all_gather.10 = bf16[1024,256]{1,0:T(8,128)(2,1)S(1)} all-gather(bf16[128,256]{1,0:T(8,128)(2,1)} %param.13), channel_id=1, replica_groups=mesh['seq'=32,'tp'=8] {'tp'}, dimensions={0}, use_global_device_ids=true | all-gather | bytes 589824 | tf_op jit(solution)/shard_map/all_gather | solution.py:88
  34.3 0.1 reshape.133
  34.4 2.7 gather_fusion
  37.0 5.0 %fusion.14 = f32[8,128,7,128]{1,3,2,0:T(8,128)} fusion(bf16[8,128,256,1]{2,1,3,0:T(8,128)(2,1)S(1)} %bitcast.149, bf16[8,7,128,256]{3,2,1,0:T(8,128)(2,1)} %bitcast.145, pred[8,7]{1,0:T(8,128)(4,1)S(1)} %copy.37), kind=kOutput, calls=%fused_computation.29 | convolution fusion | flops 471597056 | bytes 7864376 | tf_op jit(solution)/shard_map/rtd,rckd->rtck/dot_general | solution.py:120
  42.0 5.1 %copy.93 = f32[8,128,7,128]{3,2,1,0:T(8,128)} copy(f32[8,128,7,128]{1,3,2,0:T(8,128)} %fusion.14) | data formatting | bytes 7340032
  47.2 4.9 %copy.112 = f32[128,8,7,128]{3,1,2,0:T(8,128)} copy(f32[128,8,7,128]{3,2,1,0:T(8,128)} %bitcast.135) | data formatting | bytes 7340032
  52.1 1.1 copy-done.8
  53.2 0.5 copy.44
  53.8 0.6 copy.46
  54.4 0.1 copy.39
  54.6 2.9 gather_fusion.2
  57.4 23.8 %all_gather.9 = bf16[1024,256]{1,0:T(8,128)(2,1)S(1)} all-gather(bf16[128,256]{1,0:T(8,128)(2,1)S(1)} %copy-done.10), channel_id=1, replica_groups=mesh['seq'=32,'tp'=8] {'tp'}, dimensions={0}, use_global_device_ids=true | all-gather | bytes 589824 | tf_op jit(solution)/shard_map/all_gather | solution.py:87
  81.2 3.5 fusion.18
  84.7 3.9 copy.48
  88.6 0.5 copy.38
  89.1 0.6 copy.40
  89.7 2.9 gather_fusion.1
  92.7 3.5 fusion.15
  96.2 2.1 copy.42
  98.3 1.8 copy_bitcast_fusion.1
  100.1 3.7 pad_maximum_fusion
  103.9 8.4 %copy.89 = f32[1024,1792]{1,0:T(8,128)} copy(f32[1024,1792]{0,1:T(8,128)} %pad_maximum_fusion) | data formatting | bytes 14680064
  112.3 0.1 convert_reduce_fusion
  112.4 0.2 fusion.45
  112.6 43.1 %reduce-scatter.9.cloned.1.call-done = f32[32,896]{1,0:T(8,128)} async-done(((f32[1024,896]{1,0:T(8,128)}), f32[32,896]{1,0:T(8,128)}) %reduce-scatter.9.cloned.1.call-update) | async-done | bytes 114704 | tf_op jit(solution)/shard_map/reduce_scatter | solution.py:124
  155.7 118.1 %reduce-scatter.7.cloned.1.call-done = f32[32,1792]{1,0:T(8,128)} async-done(((f32[1024,1792]{1,0:T(8,128)}), f32[32,1792]{1,0:T(8,128)}) %reduce-scatter.7.cloned.1.call-update) | async-done | bytes 229392 | tf_op jit(solution)/shard_map/reduce_scatter | solution.py:20
  273.8 0.1 broadcast_in_dim.48
  273.9 1.1 multiply_convert_fusion.1
  275.0 0.7 pad_maximum_fusion.1
  275.7 0.1 broadcast_in_dim.49
  275.9 48.2 %all_to_all.15 = bf16[32,32,896]{2,1,0:T(8,128)(2,1)} all-to-all(bf16[32,32,896]{2,1,0:T(8,128)(2,1)S(1)} %broadcast_in_dim.49), channel_id=1, replica_groups=mesh['seq'=32,'tp'=8] {'seq'}, dimensions={0} | all-to-all | bytes 3670016 | tf_op jit(solution)/shard_map/all_to_all | solution.py:26
  324.1 3.7 reshape_reshape.3
  327.8 2.7 copy.67
  330.5 4.7 %fusion.29 = f32[8,128,256]{2,1,0:T(8,128)} fusion(bf16[8,128,7,128]{1,3,2,0:T(8,128)(2,1)} %copy.67, bf16[8,7,128,256]{3,2,1,0:T(8,128)(2,1)} %bitcast.146, pred[8,7]{1,0:T(8,128)(4,1)S(1)} %copy.37), kind=kOutput, calls=%fused_computation.38 | convolution fusion | flops 471597056 | bytes 6553656 | tf_op jit(solution)/shard_map/rtck,rckd->rtd/dot_general | solution.py:115
  335.2 14.4 %all-to-all-start.1 = ((f32[8,128,256]{2,1,0:T(8,128)}), f32[8,128,256]{2,1,0:T(8,128)}, u32[]{:S(2)}, u32[]{:S(2)}) async-start(f32[8,128,256]{2,1,0:T(8,128)} %fusion.29), calls=%async_computation.1 | async-start | bytes 2097152 | tf_op jit(solution)/shard_map/all_to_all | solution.py:50
  349.6 1.1 fusion.60
  350.7 6.7 %bitcast_multiply_fusion = f32[14,128,256]{2,0,1:T(8,128)S(1)} fusion(f32[8,7,128,256]{3,2,1,0:T(8,128)S(1)} %fusion.60, s32[8,14]{1,0:T(8,128)S(1)} %broadcast_add_fusion, pred[8,14]{1,0:T(8,128)(4,1)S(1)} %broadcast_compare_fusion), kind=kOutput, calls=%fused_computation.24 | convolution fusion | flops 308741664 | bytes 9175600 | tf_op jit(solution)/shard_map/toh,toye->hye/dot_general | solution.py:138
  357.4 2.3 copy.69
  359.7 8.2 %all-to-all-done.1 = f32[8,128,256]{2,1,0:T(8,128)} async-done(((f32[8,128,256]{2,1,0:T(8,128)}), f32[8,128,256]{2,1,0:T(8,128)}, u32[]{:S(2)}, u32[]{:S(2)}) %all-to-all-start.1) | async-done | bytes 1048608 | tf_op jit(solution)/shard_map/all_to_all | solution.py:50
  367.9 1.9 reduce_sum.41
  369.9 4.2 fusion.59
  374.0 3.6 reshape.161
  377.7 2.9 copy.61
  380.6 5.0 %fusion.30 = f32[8,128,256]{2,1,0:T(8,128)} fusion(bf16[8,128,7,128]{1,3,2,0:T(8,128)(2,1)} %copy.61, bf16[8,7,256,128]{3,2,1,0:T(8,128)(2,1)} %bitcast.134, pred[8,7]{1,0:T(8,128)(4,1)S(1)} %copy.37), kind=kOutput, calls=%fused_computation.39 | convolution fusion | flops 471597056 | bytes 6553656 | tf_op jit(solution)/shard_map/rtck,drck->rtd/dot_general | solution.py:156
  385.6 3.6 reshape.162
  389.3 2.7 copy.64
  392.0 5.4 %fusion.36 = f32[8,128,256]{2,1,0:T(8,128)} fusion(f32[8,128,256]{2,1,0:T(8,128)} %fusion.30, bf16[8,128,7,128]{1,3,2,0:T(8,128)(2,1)} %copy.64, bf16[8,7,256,128]{3,2,1,0:T(8,128)(2,1)} %bitcast.132, pred[8,7]{1,0:T(8,128)(4,1)S(1)} %copy.37), kind=kOutput, calls=%fused_computation.41 | convolution fusion | flops 471859200 | bytes 7602232 | tf_op jit(solution)/shard_map/rtck,drck->rtd/dot_general | solution.py:158
  397.4 4.4 all-to-all-start.2
  401.8 4.1 convolution_bitcast_fusion.1
  405.9 8.0 %copy.62 = f32[256,8,7,128]{3,1,2,0:T(8,128)} copy(f32[256,8,7,128]{0,3,2,1:T(8,128)} %convolution_bitcast_fusion.1) | data formatting | bytes 14680064 | tf_op jit(solution)/shard_map/rtd,rtck->drck/transpose | solution.py:142
  413.9 4.8 %fusion.13 = f32[256,14,128]{2,1,0:T(8,128)S(1)} fusion(f32[256,8,7,128]{3,1,2,0:T(8,128)} %copy.62, s32[8,14]{1,0:T(8,128)S(1)} %broadcast_add_fusion, pred[8,14]{1,0:T(8,128)(4,1)S(1)} %broadcast_compare_fusion), kind=kOutput, calls=%fused_computation.28 | convolution fusion | flops 308741664 | bytes 9175600 | tf_op jit(solution)/shard_map/rcb,drck->dbk/dot_general | solution.py:145
  418.7 1.8 copy.63
  420.5 2.9 copy.70
  423.3 4.1 convolution_bitcast_fusion
  427.4 8.0 %copy.65 = f32[256,8,7,128]{3,1,2,0:T(8,128)} copy(f32[256,8,7,128]{0,3,2,1:T(8,128)} %convolution_bitcast_fusion) | data formatting | bytes 14680064 | tf_op jit(solution)/shard_map/rtd,rtck->drck/transpose | solution.py:149
  435.4 4.8 %fusion.12 = f32[256,14,128]{2,1,0:T(8,128)S(1)} fusion(f32[256,8,7,128]{3,1,2,0:T(8,128)} %copy.65, s32[8,14]{1,0:T(8,128)S(1)} %broadcast_add_fusion, pred[8,14]{1,0:T(8,128)(4,1)S(1)} %broadcast_compare_fusion), kind=kOutput, calls=%fused_computation.26 | convolution fusion | flops 308741664 | bytes 9175600 | tf_op jit(solution)/shard_map/rcb,drck->dbk/dot_general | solution.py:152
  440.3 1.8 copy.66
  442.0 2.7 copy.71
  444.7 1.9 reduce_sum.42
  (37 shorter events, 0.4 us)
Async XLA Ops:
  7.2 27.2 %copy-start = (bf16[1792,256]{1,0:T(8,128)(2,1)S(1)}, bf16[1792,256]{1,0:T(8,128)(2,1)}, u32[]{:S(2)}) copy-start(bf16[1792,256]{1,0:T(8,128)(2,1)} %param.11) | copy-start | bytes 2752516
  7.2 148.5 %reduce-scatter.9.cloned.1.call-start = ((), (), s32[]{:S(2)}) async-start(), calls=%async_computation.7 | async-start | bytes 3784704 | tf_op jit(solution)/shard_map/reduce_scatter | solution.py:124
  34.3 2.8 copy-start.6
  52.0 1.2 copy-start.8
  52.1 221.8 %reduce-scatter.7.cloned.1.call-start = ((), (), s32[]{:S(2)}) async-start(), calls=%async_computation.6 | async-start | bytes 7569408 | tf_op jit(solution)/shard_map/reduce_scatter | solution.py:20
  54.6 2.9 copy-start.10
  84.7 3.9 copy-start.9
  96.2 2.1 copy-start.2
  112.3 257.6 %all-gather.2.cloned.1.call-start = ((), (), s32[]{:S(2)}) async-start(), calls=%async_computation.5 | async-start | bytes 3784704 | tf_op jit(solution)/shard_map/all_gather | solution.py:57
  330.5 19.1 %copy-start.5 = (bf16[8,128,7,128]{1,3,2,0:T(8,128)(2,1)S(1)}, bf16[8,128,7,128]{1,3,2,0:T(8,128)(2,1)}, u32[]{:S(2)}) copy-start(bf16[8,128,7,128]{1,3,2,0:T(8,128)(2,1)} %copy.67) | copy-start | bytes 5505028
  330.5 19.1 %copy-start.7 = (bf16[1024,256]{1,0:T(8,128)(2,1)S(1)}, bf16[1024,256]{1,0:T(8,128)(2,1)}, u32[]{:S(2)}) copy-start(bf16[1024,256]{1,0:T(8,128)(2,1)} %copy-done.6) | copy-start | bytes 1572868
  335.2 32.7 %all-to-all-start.1 = ((f32[8,128,256]{2,1,0:T(8,128)}), f32[8,128,256]{2,1,0:T(8,128)}, u32[]{:S(2)}, u32[]{:S(2)}) async-start(f32[8,128,256]{2,1,0:T(8,128)} %fusion.29), calls=%async_computation.1 | async-start | bytes 2097152 | tf_op jit(solution)/shard_map/all_to_all | solution.py:50
  392.0 9.8 %copy-start.4 = (bf16[8,128,7,128]{1,3,2,0:T(8,128)(2,1)S(1)}, bf16[8,128,7,128]{1,3,2,0:T(8,128)(2,1)}, u32[]{:S(2)}) copy-start(bf16[8,128,7,128]{1,3,2,0:T(8,128)(2,1)} %copy.61) | copy-start | bytes 5505028
  397.4 47.3 %all-to-all-start.2 = ((f32[8,128,256]{2,1,0:T(8,128)}), f32[8,128,256]{2,1,0:T(8,128)}, u32[]{:S(2)}, u32[]{:S(2)}) async-start(f32[8,128,256]{2,1,0:T(8,128)} %fusion.36), calls=%async_computation.2 | async-start | bytes 2097152 | tf_op jit(solution)/shard_map/all_to_all | solution.py:50
  420.5 2.9 copy-start.3
  435.4 11.3 %copy-start.1 = (bf16[1792,256]{1,0:T(8,128)(2,1)S(1)}, bf16[1792,256]{1,0:T(8,128)(2,1)}, u32[]{:S(2)}) copy-start(bf16[1792,256]{1,0:T(8,128)(2,1)} %param.11) | copy-start | bytes 2752516
Sparse Core Ops, SparseCore 0:
  52.2 103.4 reduce-scatter.8
  160.3 113.4 reduce-scatter.6
  276.4 85.6 all-gather.1
where the time goes:
time: 458 us; the launch traced here: 453 us
  waiting for transfers between devices  169 us (37%)
  blocking collectives  97 us (21%)
  local copies, waits for them, and re-layouts  89.7 us (20%)
  matrix products  52.8 us (12%)
  starting transfers between devices  19 us (4%)
  between operations  14.2 us (3%)
  other arithmetic  11.3 us (2%)
    reduce_scatter x1, waiting for transfers between devices, sent_together(): lax.psum_scatter(both, axis, scatter_dimension=dim, tiled=True)  118 us
    all_to_all x1, blocking collectives, copy_for_each(): lax.all_to_all(jnp.broadcast_to(array[None], (devices, *array.shape)), ax...  48.2 us
    reduce_scatter x1, waiting for transfers between devices, shards(): lax.psum_scatter(hidden_part, 'seq', scatter_dimension=0, tiled=True)  43.1 us
    unnamed x29, local copies, waits for them, and re-layouts  26.2 us
    all_gather x1, blocking collectives, shards(): lax.all_gather(cotangent, 'tp', axis=0, tiled=True)  25 us
    all_gather x1, blocking collectives, shards(): lax.all_gather(tokens, 'tp', axis=0, tiled=True)  23.8 us
    all_to_all x2, starting transfers between devices, sum_at_owner(): lax.all_to_all(tiles, axis, split_axis=0, concat_axis=0, tiled=True)  18.8 us
  transfers between devices with their start and end apart: 5, of which 3 were waited for; matrix products, arithmetic and copies ran while one was open for 22% of the time, Pallas kernels for 0%

commit v1 on v0

v1 whole, which is shorter than its diff:
```python
import functools

import jax
import jax.numpy as jnp
from jax import lax
from jax.experimental import pallas as pl
from jax.experimental.pallas import tpu as pltpu
from jax.sharding import Mesh, PartitionSpec as P

BLK = 128
ROWBLK = 128
KEPT_HEAVY = 7
SEQ = ("x", "zh", "core")
TP = ("zl", "y")
BF16 = jnp.bfloat16
F32 = jnp.float32
ANY = pl.BlockSpec(memory_space=pl.ANY)
VMEM = pl.BlockSpec(memory_space=pltpu.VMEM)
SMEM = pl.BlockSpec(memory_space=pltpu.SMEM)


def nt(a, b):
    return lax.dot_general(a, b, (((1,), (1,)), ((), ())), preferred_element_type=F32)


def nn(a, b):
    return jnp.dot(a, b, preferred_element_type=F32)


def rows_of(r):
    return pl.ds(pl.multiple_of(r * ROWBLK, ROWBLK), ROWBLK)


def blk_of(b):
    return pl.ds(pl.multiple_of(b * BLK, BLK), BLK)


def partials_kernel(capacity, feat, first_ref, masks, own, other, gate_own, gate_other, up_own, up_other,
                    down_own, down_other, out):
    row_blocks, blocks = masks.shape
    first = first_ref[0]

    def pair(k, count):
        r, b = k // blocks, k % blocks
        at = count - first

        @pl.when((masks[r, b] == 1) & (at >= 0) & (at < capacity))
        def _():
            rows, cols = rows_of(r), blk_of(b)
            act = nn(own[rows, :feat], jnp.concatenate([gate_own[:, cols], up_own[:, cols]], axis=1))
            act += nn(other[rows, :feat], jnp.concatenate([gate_other[:, cols], up_other[:, cols]], axis=1))
            grad = nt(own[rows, feat:], down_own[cols, :]) + nt(other[rows, feat:], down_other[cols, :])
            out[rows_of(at), : 2 * BLK] = act.astype(out.dtype)
            out[rows_of(at), 2 * BLK :] = grad.astype(out.dtype)

        return count + masks[r, b]

    total = lax.fori_loop(0, row_blocks * blocks, pair, 0)

    def empty(k, c):
        out[rows_of(k), :] = jnp.zeros((ROWBLK, 3 * BLK), out.dtype)
        return c

    lax.fori_loop(jnp.clip(total - first, 0, capacity), capacity, empty, 0)


def load_acts(core, own, other, acts, sems):
    half = own.shape[0]
    mine = pltpu.make_async_copy(own, acts.at[pl.ds(pl.multiple_of(core * half, half), half)], sems.at[0])
    rest = pltpu.make_async_copy(other, acts.at[pl.ds(pl.multiple_of((1 - core) * half, half), half)], sems.at[1])
    mine.start()
    rest.start()
    mine.wait()
    rest.wait()


def rows_kernel(core_ref, masks, own, other, gate, up, down, out, acts, sems):
    row_blocks, blocks = masks.shape
    feat = down.shape[1]
    load_acts(core_ref[0], own, other, acts, sems)

    def row(r, count):
        def block(b, carry):
            count = carry[0]

            def live(count, fwd, bwd):
                act = acts[rows_of(count), :]
                cols = blk_of(b)
                fwd = fwd + nn(act[:, :BLK], down[cols, :])
                bwd = bwd + nt(act[:, BLK : 2 * BLK], gate[:, cols]) + nt(act[:, 2 * BLK :], up[:, cols])
                return count + 1, fwd, bwd

            return lax.cond(masks[r, b] == 1, live, lambda *c: c, *carry)

        zero = jnp.zeros((ROWBLK, feat), F32)
        count, fwd, bwd = lax.fori_loop(0, blocks, block, (count, zero, zero))
        out[rows_of(r), :feat] = fwd.astype(out.dtype)
        out[rows_of(r), feat:] = bwd.astype(out.dtype)
        return count

    lax.fori_loop(0, row_blocks, row, 0)


def weights_kernel(scale, core_ref, masks, own, other, rows, grad_gate, grad_up, grad_down, acts, turned, where, sems):
    row_blocks, blocks = masks.shape
    feat = grad_down.shape[1]
    b = pl.program_id(0)

    @pl.when(b == 0)
    def _():
        load_acts(core_ref[0], own, other, acts, sems)

        def pair(k, count):
            where[k] = count
            return count + masks[k // blocks, k % blocks]

        lax.fori_loop(0, row_blocks * blocks, pair, 0)
        for r in range(row_blocks):
            turned[:, r * ROWBLK : (r + 1) * ROWBLK] = rows[r * ROWBLK : (r + 1) * ROWBLK, :feat].T

    grad_gate[...] = jnp.zeros_like(grad_gate)
    grad_up[...] = jnp.zeros_like(grad_up)
    grad_down[...] = jnp.zeros_like(grad_down)
    for r in range(row_blocks):

        @pl.when(masks[r, b] == 1)
        def _():
            act = acts[rows_of(where[r * blocks + b]), :]
            both = nn(turned[:, r * ROWBLK : (r + 1) * ROWBLK], act[:, BLK:])
            grad_gate[...] += both[:, :BLK]
            grad_up[...] += both[:, BLK:]
            grad_down[...] += nn(act[:, :BLK].T, rows[r * ROWBLK : (r + 1) * ROWBLK, feat:])

    grad_gate[...] *= scale
    grad_up[...] *= scale
    grad_down[...] *= scale


def copies(array, axis):
    n = lax.axis_size(axis)
    return lax.all_to_all(jnp.broadcast_to(array[None], (n, *array.shape)), axis, 0, 0, tiled=True)


def across(array):
    return lax.ppermute(array, "core", [(0, 1), (1, 0)])


def summed(array, axis):
    n = lax.axis_size(axis)
    tiles = array.reshape(n, array.shape[0] // n, array.shape[1])
    return lax.all_to_all(tiles, axis, 0, 0, tiled=True).astype(F32).sum(axis=0)


def shards(tokens, gate, up, down, masks, cotangent):
    own_rows, feat = tokens.shape
    row_blocks, blocks = masks.shape
    capacity = row_blocks * KEPT_HEAVY
    half = capacity // 2
    core = lax.axis_index("core").astype(jnp.int32)[None]
    params = pltpu.CompilerParams(vmem_limit_bytes=40 << 20)

    gate_other, up_other, down_other = across(gate), across(up), across(down)
    rows = copies(jnp.concatenate([tokens, cotangent], axis=1), TP).reshape(-1, 2 * feat)
    rows_other = across(rows)

    parts = pl.pallas_call(
        functools.partial(partials_kernel, half, feat),
        out_shape=jax.ShapeDtypeStruct((half * ROWBLK, 3 * BLK), BF16),
        in_specs=[SMEM, SMEM] + [VMEM] * 8,
        out_specs=VMEM,
        compiler_params=params,
        name="partials",
    )(core * half, masks, rows, rows_other, gate, gate_other, up, up_other, down, down_other)

    sums = summed(summed(parts, "x"), "zh")
    gate_act, up_act, grad_hidden = sums[:, :BLK], sums[:, BLK : 2 * BLK], sums[:, 2 * BLK :]
    s = jax.nn.sigmoid(gate_act)
    acts = jnp.concatenate(
        [
            (jax.nn.silu(gate_act) * up_act).astype(BF16),
            (grad_hidden * up_act * s * (1.0 + gate_act * (1.0 - s))).astype(BF16),
            (grad_hidden * gate_act * s).astype(BF16),
        ],
        axis=1,
    )
    acts = copies(acts, "zh").reshape(-1, 3 * BLK)
    acts = copies(acts, "x").reshape(-1, 3 * BLK)
    acts_other = across(acts)

    scratch = [pltpu.VMEM((capacity * ROWBLK, 3 * BLK), BF16)]
    partial_rows = pl.pallas_call(
        rows_kernel,
        out_shape=jax.ShapeDtypeStruct((row_blocks * ROWBLK, 2 * feat), BF16),
        in_specs=[SMEM, SMEM, ANY, ANY, VMEM, VMEM, VMEM],
        out_specs=VMEM,
        scratch_shapes=scratch + [pltpu.SemaphoreType.DMA((2,))],
        compiler_params=params,
        name="row_grads",
    )(core, masks, acts, acts_other, gate, up, down)
    out_rows = summed(partial_rows, TP).astype(BF16)

    columns = pl.BlockSpec((feat, BLK), lambda b: (0, b))
    grad_gate, grad_up, grad_down = pl.pallas_call(
        functools.partial(weights_kernel, (row_blocks * ROWBLK) ** -0.5),
        grid=(blocks,),
        out_shape=(
            jax.ShapeDtypeStruct(gate.shape, F32),
            jax.ShapeDtypeStruct(up.shape, F32),
            jax.ShapeDtypeStruct(down.shape, F32),
        ),
        in_specs=[SMEM, SMEM, ANY, ANY, VMEM],
        out_specs=(columns, columns, pl.BlockSpec((BLK, feat), lambda b: (b, 0))),
        scratch_shapes=scratch
        + [
            pltpu.VMEM((feat, row_blocks * ROWBLK), BF16),
            pltpu.SMEM((row_blocks * blocks,), jnp.int32),
            pltpu.SemaphoreType.DMA((2,)),
        ],
        compiler_params=params,
        name="weight_grads",
    )(core, masks, acts, acts_other, rows)
    return out_rows[:, :feat], out_rows[:, feat:], grad_gate, grad_up, grad_down


def solution(mesh):
    fine = Mesh(mesh.devices.reshape(4, 4, 2, 2, 4), SEQ + TP)
    wide, tall = P(SEQ, TP), P(TP, SEQ)
    return jax.shard_map(
        shards,
        mesh=fine,
        in_specs=(tall, wide, wide, tall, P(None, TP), tall),
        out_specs=(tall, tall, wide, wide, tall),
        check_vma=False,
    )
```

time: 458 us -> 215 us (0.47); the launches traced: 453 us -> 215 us
  waiting for transfers between devices: 169 us -> 10.5 us
  local copies, waits for them, and re-layouts: 89.7 us -> 5.04 us
  blocking collectives: 97 us -> 150 us
  matrix products: 52.8 us -> 0 us
  Pallas kernels: 0 us -> 35.6 us
  between operations: 14.2 us -> 0.81 us
  starting transfers between devices: 19 us -> 9.91 us
  other arithmetic: 11.3 us -> 3 us
    reduce_scatter x2 -> x0, waiting for transfers between devices: 161 us -> none  [the longest x1 118 us: sent_together(): lax.psum_scatter(both, axis, scatter_dimension=dim, tiled=True)]
    all_to_all x1 -> x5, blocking collectives: 48.2 us -> 150 us  [the longest x3 75.5 us: copies(): lax.all_to_all(jnp.broadcast_to(array[None], (n, *array.shape)), axis, 0,...]
    dot_general x13 -> x0, matrix products: 52.8 us -> none  [the longest x1 6.7 us: shards(): jnp.einsum('toh,toye->hye', slot_indicator, down_compact, precision=lax.P...]
    all_gather x2 -> x0, blocking collectives: 48.8 us -> none  [the longest x1 25 us: shards(): lax.all_gather(cotangent, 'tp', axis=0, tiled=True)]
    pallas_call x0 -> x3, Pallas kernels: none -> 35.6 us  [the longest x1 14.7 us: shards(): pl.pallas_call(rows_kernel, out_shape=jax.ShapeDtypeStruct((row_blocks *...]
    unnamed x29 -> x20, local copies, waits for them, and re-layouts: 26.2 us -> 4 us
    transpose x2 -> x0, local copies, waits for them, and re-layouts: 16.1 us -> none  [the longest x1 8.04 us: shards(): jnp.einsum('rtd,rtck->drck', token_blocks, up_act_blocks, preferred_eleme...]
    reshape x7 -> x0, local copies, waits for them, and re-layouts: 16 us -> none  [the longest x2 6.58 us: shards(): gate_act_blocks = grad_gate_act.reshape(row_blocks, ROWBLK, capacity, BLK)]
  transfers between devices with their start and end apart: 5 -> 6, of which waited for: 3 -> 3; matrix products, arithmetic and copies ran while one was open for 22% -> 0% of each run, Pallas kernels for 0% -> 7%
where the time goes in v1:
time: 215 us
  blocking collectives  150 us (70%)
  Pallas kernels  35.6 us (17%)
  waiting for transfers between devices  10.5 us (5%)
  starting transfers between devices  9.91 us (5%)
  local copies, waits for them, and re-layouts  5.04 us (2%)
  other arithmetic  3 us (1%)
    all_to_all x3, blocking collectives, copies(): lax.all_to_all(jnp.broadcast_to(array[None], (n, *array.shape)), axis, 0,...  75.5 us
    all_to_all x2, blocking collectives, summed(): return lax.all_to_all(tiles, axis, 0, 0, tiled=True).astype(F32).sum(axis=0)  74.9 us
    pallas_call x1, Pallas kernels, shards(): pl.pallas_call(rows_kernel, out_shape=jax.ShapeDtypeStruct((row_blocks *...  14.7 us
    pallas_call x1, Pallas kernels, shards(): pl.pallas_call(functools.partial(weights_kernel, (row_blocks * ROWBLK) **...  14.3 us
    ppermute x5, waiting for transfers between devices, across(): return lax.ppermute(array, 'core', [(0, 1), (1, 0)])  10.5 us
    pallas_call x1, Pallas kernels, shards(): pl.pallas_call(functools.partial(partials_kernel, half, feat), out_shape=...  6.61 us
    ppermute x5, starting transfers between devices, across(): return lax.ppermute(array, 'core', [(0, 1), (1, 0)])  5.67 us
  transfers between devices with their start and end apart: 6, of which 3 were waited for; matrix products, arithmetic and copies ran while one was open for 0% of the time, Pallas kernels for 7%

profile of v1, /device:TPU:1, one launch (start us, length us, event | category | flops | bytes accessed | tf_op | source)
XLA Modules:
  0.0 215.3 jit_solution(16992596354201694010)
XLA Ops:
  0.6 0.0 copy-start.5
  0.6 0.0 copy-start.7
  0.7 0.0 copy-start.9
  0.7 1.0 pad_maximum_fusion.1
  1.7 0.1 broadcast_in_dim.11
  1.8 20.5 %all_to_all.30 = bf16[8,128,512]{2,1,0:T(8,128)(2,1)S(1)} all-to-all(bf16[8,128,512]{2,1,0:T(8,128)(2,1)S(1)} %broadcast_in_dim.11), channel_id=1, replica_groups=mesh['x'=4,'zh'=4,'core'=2,'zl'=2,'y'=4] {'zl','y'}, dimensions={0} | all-to-all | bytes 2097152 | tf_op jit(solution)/shard_map/all_to_all | solution.py:141
  22.2 0.0 copy-start.2
  22.2 2.4 %collective-permute-start = (bf16[1024,512]{1,0:T(8,128)(2,1)S(1)}, bf16[1024,512]{1,0:T(8,128)(2,1)}, u32[]{:S(2)}, u32[]{:S(2)}) collective-permute-start(bf16[1024,512]{1,0:T(8,128)(2,1)S(1)} %bitcast.11), channel_id=1, source_target_pairs={{0,8},{8,0},{1,9},{9,1},{2,10},{10,2},{3,11},{11,3},{4,12},{12,4},... | collective-permute-start | bytes 3145736 | tf_op jit(solution)/shard_map/ppermute | solution.py:145
  24.7 0.0 copy-done.5
  24.7 0.1 collective-permute-start.1
  24.8 0.0 copy-done.7
  24.8 0.4 collective-permute-start.2
  25.2 0.1 collective-permute-start.3
  25.3 4.4 %collective-permute-done.1.gate_other = bf16[256,1792]{1,0:T(8,128)(2,1)} collective-permute-done((bf16[256,1792]{1,0:T(8,128)(2,1)S(1)}, bf16[256,1792]{1,0:T(8,128)(2,1)}, u32[]{:S(2)}, u32[]{:S(2)}) %collective-permute-start.1) | collective-permute-done | bytes 917536 | tf_op jit(solution)/shard_map/ppermute | solution.py:145
  29.7 1.3 collective-permute-done.2.up_other
  31.0 0.0 collective-permute-done.3.down_other
  31.0 0.0 collective-permute-done.other
  31.0 0.0 copy-done.9
  31.0 6.6 %partials.1 = bf16[3584,384]{1,0:T(8,128)(2,1)S(1)} custom-call(s32[1]{0:T(128)S(6)} %mul.28.first_ref, s32[8,14]{1,0:T(8,128)S(1)} %copy-done.9, bf16[1024,512]{1,0:T(8,128)(2,1)S(1)} %bitcast.12, bf16[1024,512]{1,0:T(8,128)(2,1)} %collective-permute-done.other, bf16[256,1792]{1,0:T(8,128)(2,1)S(1)} %copy-done.5, ...), custom_call_target="tpu_custom_call" | custom-call | tf_op jit(solution)/shard_map/partials/pallas_call | solution.py:166
  37.7 0.0 copy-done.2
  37.7 31.3 %all_to_all.31 = bf16[4,896,384]{2,1,0:T(8,128)(2,1)S(1)} all-to-all(bf16[4,896,384]{2,1,0:T(8,128)(2,1)S(1)} %bitcast.10), channel_id=1, replica_groups=mesh['x'=4,'zh'=4,'core'=2,'zl'=2,'y'=4] {'x'}, dimensions={0} | all-to-all | bytes 5505024 | tf_op jit(solution)/shard_map/all_to_all | solution.py:151
  69.0 0.4 convert_reduce_fusion
  69.4 43.6 %all_to_all.32 = f32[4,224,384]{2,1,0:T(8,128)S(1)} all-to-all(f32[4,224,384]{2,1,0:T(8,128)S(1)} %bitcast.15), channel_id=1, replica_groups=mesh['x'=4,'zh'=4,'core'=2,'zl'=2,'y'=4] {'zh'}, dimensions={0} | all-to-all | bytes 2752512 | tf_op jit(solution)/shard_map/all_to_all | solution.py:151
  113.0 0.1 reduce_sum.31
  113.1 0.1 multiply_convert_fusion.2
  113.2 0.1 broadcast_in_dim.24
  113.3 20.7 %all_to_all.33 = bf16[4,224,384]{2,1,0:T(8,128)(2,1)S(1)} all-to-all(bf16[4,224,384]{2,1,0:T(8,128)(2,1)S(1)} %broadcast_in_dim.24), channel_id=1, replica_groups=mesh['x'=4,'zh'=4,'core'=2,'zl'=2,'y'=4] {'zh'}, dimensions={0} | all-to-all | bytes 1376256 | tf_op jit(solution)/shard_map/all_to_all | solution.py:141
  134.0 0.2 broadcast_in_dim.26
  134.3 0.0 copy-start.6
  134.3 0.0 copy-start.8
  134.3 34.3 %all_to_all.34 = bf16[4,896,384]{2,1,0:T(8,128)(2,1)S(1)} all-to-all(bf16[4,896,384]{2,1,0:T(8,128)(2,1)S(1)} %broadcast_in_dim.26), channel_id=1, replica_groups=mesh['x'=4,'zh'=4,'core'=2,'zl'=2,'y'=4] {'x'}, dimensions={0} | all-to-all | bytes 5505024 | tf_op jit(solution)/shard_map/all_to_all | solution.py:141
  168.6 2.6 %collective-permute-start.4 = (bf16[3584,384]{1,0:T(8,128)(2,1)S(1)}, bf16[3584,384]{1,0:T(8,128)(2,1)S(1)}, u32[]{:S(2)}, u32[]{:S(2)}) collective-permute-start(bf16[3584,384]{1,0:T(8,128)(2,1)S(1)} %bitcast.7), channel_id=1, source_target_pairs={{0,8},{8,0},{1,9},{9,1},{2,10},{10,2},{3,11},{11,3},{4,12},{12,4},... | collective-permute-start | bytes 8257544 | tf_op jit(solution)/shard_map/ppermute | solution.py:145
  171.2 4.7 %collective-permute-done.4.other = bf16[3584,384]{1,0:T(8,128)(2,1)S(1)} collective-permute-done((bf16[3584,384]{1,0:T(8,128)(2,1)S(1)}, bf16[3584,384]{1,0:T(8,128)(2,1)S(1)}, u32[]{:S(2)}, u32[]{:S(2)}) %collective-permute-start.4) | collective-permute-done | bytes 2752544 | tf_op jit(solution)/shard_map/ppermute | solution.py:145
  175.9 0.0 copy-done.6
  175.9 0.0 copy-done.8
  175.9 0.0 copy-start
  175.9 14.7 %row_grads.1 = bf16[1024,512]{1,0:T(8,128)(2,1)S(1)} custom-call(s32[1]{0:T(128)} %bitcast.core_ref, s32[8,14]{1,0:T(8,128)S(1)} %copy-done.9, bf16[3584,384]{1,0:T(8,128)(2,1)S(1)} %bitcast.8, bf16[3584,384]{1,0:T(8,128)(2,1)S(1)} %collective-permute-done.4.other, bf16[256,1792]{1,0:T(8,128)(2,1)S(1)} %copy-done.6, bf16[256,1792]{1,0:T(8,128)(2,1)S(1)} %copy-done.8, ...), custom_call_target="tpu_custom_call" | custom-call | tf_op jit(solution)/shard_map/row_grads/pallas_call | solution.py:191
  190.7 0.0 copy-done
  190.7 0.0 copy-start.4
  190.7 1.0 copy-done.4
  191.7 4.2 %all-to-all-start.5 = ((bf16[8,128,512]{2,1,0:T(8,128)(2,1)}), bf16[8,128,512]{2,1,0:T(8,128)(2,1)}, u32[]{:S(2)}, u32[]{:S(2)}) async-start(bf16[8,128,512]{2,1,0:T(8,128)(2,1)} %bitcast.14), calls=%async_computation.5 | async-start | bytes 2097152 | tf_op jit(solution)/shard_map/all_to_all | solution.py:151
  195.9 0.0 copy-start.1
  195.9 1.8 copy-done.1
  197.7 0.0 copy-start.3
  197.7 1.2 copy-done.3
  198.9 14.3 %weight_grads.1 = (f32[256,1792]{1,0:T(8,128)}, f32[256,1792]{1,0:T(8,128)}, f32[1792,256]{1,0:T(8,128)}) custom-call(s32[1]{0:T(128)} %bitcast.core_ref, s32[8,14]{1,0:T(8,128)S(1)} %copy-done.9, bf16[3584,384]{1,0:T(8,128)(2,1)S(1)} %bitcast.9, bf16[3584,384]{1,0:T(8,128)(2,1)S(1)} %copy-done.1, bf16[1024,512]{1,0:T(8,128)(2,1)S(1)} %bitcast.13), custom_call_target="tpu_custom_call" | custom-call | tf_op jit(solution)/shard_map/weight_grads/pallas_call | solution.py:203
  213.2 0.0 all-to-all-done.5
  213.2 1.4 reduce_sum.32
  214.6 0.7 fusion
  (1 shorter events, 0.0 us)
Async XLA Ops:
  0.6 24.0 %copy-start.5 = (bf16[256,1792]{1,0:T(8,128)(2,1)S(1)}, bf16[256,1792]{1,0:T(8,128)(2,1)}, u32[]{:S(2)}) copy-start(bf16[256,1792]{1,0:T(8,128)(2,1)} %gate.1) | copy-start | bytes 2752516
  0.6 24.1 %copy-start.7 = (bf16[256,1792]{1,0:T(8,128)(2,1)S(1)}, bf16[256,1792]{1,0:T(8,128)(2,1)}, u32[]{:S(2)}) copy-start(bf16[256,1792]{1,0:T(8,128)(2,1)} %up.1) | copy-start | bytes 2752516
  0.7 30.4 %copy-start.9 = (s32[8,14]{1,0:T(8,128)S(1)}, s32[8,14]{1,0:T(8,128)}, u32[]{:S(2)}) copy-start(s32[8,14]{1,0:T(8,128)} %masks.5) | copy-start | bytes 1348
  22.2 15.4 %copy-start.2 = (bf16[8,128,512]{2,1,0:T(8,128)(2,1)}, bf16[8,128,512]{2,1,0:T(8,128)(2,1)S(1)}, u32[]{:S(2)}) copy-start(bf16[8,128,512]{2,1,0:T(8,128)(2,1)S(1)} %all_to_all.30) | copy-start | bytes 3145732
  22.2 8.8 %collective-permute-start = (bf16[1024,512]{1,0:T(8,128)(2,1)S(1)}, bf16[1024,512]{1,0:T(8,128)(2,1)}, u32[]{:S(2)}, u32[]{:S(2)}) collective-permute-start(bf16[1024,512]{1,0:T(8,128)(2,1)S(1)} %bitcast.11), channel_id=1, source_target_pairs={{0,8},{8,0},{1,9},{9,1},{2,10},{10,2},{3,11},{11,3},{4,12},{12,4},... | collective-permute-start | bytes 3145736 | tf_op jit(solution)/shard_map/ppermute | solution.py:145
  24.7 5.0 %collective-permute-start.1 = (bf16[256,1792]{1,0:T(8,128)(2,1)S(1)}, bf16[256,1792]{1,0:T(8,128)(2,1)}, u32[]{:S(2)}, u32[]{:S(2)}) collective-permute-start(bf16[256,1792]{1,0:T(8,128)(2,1)S(1)} %copy-done.5), channel_id=1, source_target_pairs={{0,8},{8,0},{1,9},{9,1},{2,10},{10,2},{3,11},{11,3},{4,12},{12,4},... | collective-permute-start | bytes 2752520 | tf_op jit(solution)/shard_map/ppermute | solution.py:145
  24.8 6.3 %collective-permute-start.2 = (bf16[256,1792]{1,0:T(8,128)(2,1)S(1)}, bf16[256,1792]{1,0:T(8,128)(2,1)}, u32[]{:S(2)}, u32[]{:S(2)}) collective-permute-start(bf16[256,1792]{1,0:T(8,128)(2,1)S(1)} %copy-done.7), channel_id=1, source_target_pairs={{0,8},{8,0},{1,9},{9,1},{2,10},{10,2},{3,11},{11,3},{4,12},{12,4},... | collective-permute-start | bytes 2752520 | tf_op jit(solution)/shard_map/ppermute | solution.py:145
  25.2 5.8 %collective-permute-start.3 = (bf16[1792,256]{1,0:T(8,128)(2,1)}, bf16[1792,256]{1,0:T(8,128)(2,1)}, u32[]{:S(2)}, u32[]{:S(2)}) collective-permute-start(bf16[1792,256]{1,0:T(8,128)(2,1)} %down.1), channel_id=1, source_target_pairs={{0,8},{8,0},{1,9},{9,1},{2,10},{10,2},{3,11},{11,3},{4,12},{12,4},... | collective-permute-start | bytes 2752520 | tf_op jit(solution)/shard_map/ppermute | solution.py:145
  134.3 41.7 %copy-start.6 = (bf16[256,1792]{1,0:T(8,128)(2,1)S(1)}, bf16[256,1792]{1,0:T(8,128)(2,1)}, u32[]{:S(2)}) copy-start(bf16[256,1792]{1,0:T(8,128)(2,1)} %gate.1) | copy-start | bytes 2752516
  134.3 41.7 %copy-start.8 = (bf16[256,1792]{1,0:T(8,128)(2,1)S(1)}, bf16[256,1792]{1,0:T(8,128)(2,1)}, u32[]{:S(2)}) copy-start(bf16[256,1792]{1,0:T(8,128)(2,1)} %up.1) | copy-start | bytes 2752516
  168.6 7.4 %collective-permute-start.4 = (bf16[3584,384]{1,0:T(8,128)(2,1)S(1)}, bf16[3584,384]{1,0:T(8,128)(2,1)S(1)}, u32[]{:S(2)}, u32[]{:S(2)}) collective-permute-start(bf16[3584,384]{1,0:T(8,128)(2,1)S(1)} %bitcast.7), channel_id=1, source_target_pairs={{0,8},{8,0},{1,9},{9,1},{2,10},{10,2},{3,11},{11,3},{4,12},{12,4},... | collective-permute-start | bytes 8257544 | tf_op jit(solution)/shard_map/ppermute | solution.py:145
  175.9 14.7 %copy-start = (bf16[3584,384]{1,0:T(8,128)(2,1)}, bf16[3584,384]{1,0:T(8,128)(2,1)S(1)}, u32[]{:S(2)}) copy-start(bf16[3584,384]{1,0:T(8,128)(2,1)S(1)} %collective-permute-done.4.other) | copy-start | bytes 8257540
  190.7 1.0 copy-start.4
  191.7 21.6 %all-to-all-start.5 = ((bf16[8,128,512]{2,1,0:T(8,128)(2,1)}), bf16[8,128,512]{2,1,0:T(8,128)(2,1)}, u32[]{:S(2)}, u32[]{:S(2)}) async-start(bf16[8,128,512]{2,1,0:T(8,128)(2,1)} %bitcast.14), calls=%async_computation.5 | async-start | bytes 2097152 | tf_op jit(solution)/shard_map/all_to_all | solution.py:151
  195.9 1.8 copy-start.1
  197.7 1.2 copy-start.3

commit v2 on v1

v2 whole, which is shorter than its diff:
```python
import functools

import jax
import jax.numpy as jnp
from jax import lax
from jax.experimental import pallas as pl
from jax.experimental.pallas import tpu as pltpu
from jax.sharding import Mesh, PartitionSpec as P

BLK = 128
ROWBLK = 128
BASE = 3
EXTRA = 4
UNITS = 4
SEQ = ("x", "zh", "core")
TP = ("zl", "y")
BF16 = jnp.bfloat16
F32 = jnp.float32
ANY = pl.BlockSpec(memory_space=pl.ANY)
VMEM = pl.BlockSpec(memory_space=pltpu.VMEM)
SMEM = pl.BlockSpec(memory_space=pltpu.SMEM)
PARAMS = pltpu.CompilerParams(vmem_limit_bytes=40 << 20)


def nt(a, b):
    return lax.dot_general(a, b, (((1,), (1,)), ((), ())), preferred_element_type=F32)


def nn(a, b):
    return jnp.dot(a, b, preferred_element_type=F32)


def tile(i):
    if isinstance(i, int):
        return pl.ds(i * BLK, BLK)
    return pl.ds(pl.multiple_of(i * BLK, BLK), BLK)


class Table:
    def __init__(self, rows, blocks):
        self.rows, self.blocks = rows, blocks
        self.base = 0
        self.extra = self.base + BASE * rows
        self.unit_row = self.extra + EXTRA * rows
        self.row_unit = self.unit_row + rows
        self.live_row = self.row_unit + rows
        self.live_at = self.live_row + rows * blocks
        self.live = self.live_at + rows * blocks
        self.units = self.live + blocks
        self.spare = self.units + 1
        self.size = self.spare + 1
        self.pairs = (BASE + EXTRA) * rows


def table_kernel(t, masks, out):
    def clear(k, c):
        out[k] = 0
        return c

    def none(k, c):
        out[t.live_at + k] = t.pairs
        return c

    lax.fori_loop(0, t.size, clear, 0)
    lax.fori_loop(0, t.rows * t.blocks, none, 0)

    def row(r, units):
        def block(b, count):
            kept = masks[r, b] == 1
            based = count < BASE
            at = jnp.where(based, BASE * r + count, BASE * t.rows + EXTRA * units + count - BASE)
            slot = jnp.where(based, t.base + at, t.extra + at - BASE * t.rows)
            out[jnp.where(kept, slot, t.spare)] = b
            live = t.rows * b + out[t.live + b]
            out[jnp.where(kept, t.live_row + live, t.spare)] = r
            out[jnp.where(kept, t.live_at + live, t.spare)] = at
            out[t.live + b] = out[t.live + b] + masks[r, b]
            return count + masks[r, b]

        count = lax.fori_loop(0, t.blocks, block, 0)
        heavy = count > BASE
        out[t.row_unit + r] = jnp.where(heavy, units, -1)
        out[jnp.where(heavy, t.unit_row + units, t.spare)] = r
        return units + heavy.astype(jnp.int32)

    out[t.units] = lax.fori_loop(0, t.rows, row, 0)


def partials_kernel(t, feat, first_unit, with_base, core_ref, table, own, other, gate_own, gate_other, up_own, up_other,
                    down_own, down_other, out):
    core = core_ref[0]
    before = 0

    def products(at, row, picks):
        rows = tile(row)
        for j, b in enumerate(picks):
            cols = tile(b)
            act = nn(own[rows, :feat], jnp.concatenate([gate_own[:, cols], up_own[:, cols]], axis=1))
            act += nn(other[rows, :feat], jnp.concatenate([gate_other[:, cols], up_other[:, cols]], axis=1))
            grad = nt(own[rows, feat:], down_own[cols, :]) + nt(other[rows, feat:], down_other[cols, :])
            out[tile(at + j), : 2 * BLK] = act.astype(out.dtype)
            out[tile(at + j), 2 * BLK :] = grad.astype(out.dtype)

    if with_base:
        per_core = t.rows // 2
        for i in range(per_core):
            r = core * per_core + i
            products(BASE * i, r, [table[t.base + BASE * r + j] for j in range(BASE)])
        before = BASE * per_core
    per_core = UNITS // 2
    for i in range(per_core):
        u = first_unit + core * per_core + i
        picks = [table[t.extra + EXTRA * u + j] for j in range(EXTRA)]
        products(before + EXTRA * i, table[t.unit_row + u], picks)


def load_acts(t, core, table, halves, acts, sems):
    base, main = BASE * t.rows, BASE * t.rows + EXTRA * UNITS

    def copies_of(moves):
        for k, (ref, skip, at, size, whose) in enumerate(moves):
            start = pl.multiple_of((at + whose * size) * BLK, BLK)
            yield pltpu.make_async_copy(ref.at[pl.ds(skip * BLK, size * BLK)], acts.at[pl.ds(start, size * BLK)], sems.at[k])

    def move(moves):
        for copy in copies_of(moves):
            copy.start()
        for copy in copies_of(moves):
            copy.wait()

    def both(skip, at, size, own, other):
        return [(own, skip, at, size, core), (other, skip, at, size, 1 - core)]

    units = EXTRA * UNITS // 2
    move(both(0, 0, base // 2, *halves[:2]) + both(base // 2, base, units, *halves[:2]))

    @pl.when(table[t.units] > UNITS)
    def _():
        move(both(0, main, units, *halves[2:]))


def rows_kernel(t, core_ref, table, *refs):
    halves, (gate, up, down, out, acts, total, sems) = refs[:4], refs[4:]
    feat = down.shape[1]
    load_acts(t, core_ref[0], table, halves, acts, sems)

    def products(at, picks):
        fwd, bwd = 0.0, 0.0
        for j, b in enumerate(picks):
            act, cols = acts[tile(at + j), :], tile(b)
            fwd += nn(act[:, :BLK], down[cols, :])
            bwd += nt(act[:, BLK:], jnp.concatenate([gate[:, cols], up[:, cols]], axis=1))
        return fwd, bwd

    for r in range(t.rows):
        fwd, bwd = products(BASE * r, [table[t.base + BASE * r + j] for j in range(BASE)])
        total[r, :, :feat] = fwd
        total[r, :, feat:] = bwd
        u = table[t.row_unit + r]

        @pl.when(u >= 0)
        def _():
            fwd, bwd = products(BASE * t.rows + EXTRA * u, [table[t.extra + EXTRA * u + j] for j in range(EXTRA)])
            total[r, :, :feat] += fwd
            total[r, :, feat:] += bwd

    for r in range(t.rows):
        out[tile(r), :] = total[r].astype(out.dtype)


def weights_kernel(t, together, scale, core_ref, table, *refs):
    halves, (rows, grad_gate, grad_up, grad_down, acts, turned, sems) = refs[:4], refs[4:]
    feat = grad_down.shape[1]
    step = pl.program_id(0)

    @pl.when(step == 0)
    def _():
        load_acts(t, core_ref[0], table, halves, acts, sems)
        acts[tile(t.pairs), :] = jnp.zeros((BLK, acts.shape[1]), acts.dtype)
        for r in range(t.rows):
            turned[:, tile(r)] = rows[tile(r), :feat].T

    for i in range(together):
        b = step * together + i

        def two(j):
            live = t.rows * b + j
            picked = [table[t.live_row + live], table[t.live_row + live + 1]]
            act = jnp.concatenate([acts[tile(table[t.live_at + live + k]), :] for k in (0, 1)], axis=0)
            both = nn(jnp.concatenate([turned[:, tile(r)] for r in picked], axis=1), act[:, BLK:])
            cot = jnp.concatenate([rows[tile(r), feat:] for r in picked], axis=0)
            down = nn(act[:, :BLK].T, cot)
            return both[:, :BLK] * scale, both[:, BLK:] * scale, down * scale

        grad_gate[:, tile(i)], grad_up[:, tile(i)], grad_down[tile(i), :] = two(0)
        for j in range(2, t.rows, 2):

            @pl.when(table[t.live + b] > j)
            def _():
                gate, up, down = two(j)
                grad_gate[:, tile(i)] += gate
                grad_up[:, tile(i)] += up
                grad_down[tile(i), :] += down


def copies(array, axis):
    n = lax.axis_size(axis)
    return lax.all_to_all(jnp.broadcast_to(array[None], (n, *array.shape)), axis, 0, 0, tiled=True)


def across(array):
    return lax.ppermute(array, "core", [(0, 1), (1, 0)])


def summed(array, axis):
    n = lax.axis_size(axis)
    tiles = array.reshape(n, array.shape[0] // n, array.shape[1])
    return lax.all_to_all(tiles, axis, 0, 0, tiled=True).astype(F32).sum(axis=0)


def activations(parts):
    sums = summed(summed(parts, "x"), "zh")
    gate, up, grad = sums[:, :BLK], sums[:, BLK : 2 * BLK], sums[:, 2 * BLK :]
    s = jax.nn.sigmoid(gate)
    acts = jnp.concatenate(
        [
            (jax.nn.silu(gate) * up).astype(BF16),
            (grad * up * s * (1.0 + gate * (1.0 - s))).astype(BF16),
            (grad * gate * s).astype(BF16),
        ],
        axis=1,
    )
    acts = copies(acts, "zh").reshape(-1, 3 * BLK)
    acts = copies(acts, "x").reshape(-1, 3 * BLK)
    return acts, across(acts)


def shards(tokens, gate, up, down, masks, cotangent):
    feat = tokens.shape[1]
    row_blocks, blocks = masks.shape
    t = Table(row_blocks, blocks)
    core = lax.axis_index("core").astype(jnp.int32)[None]

    table = pl.pallas_call(
        functools.partial(table_kernel, t),
        out_shape=jax.ShapeDtypeStruct((t.size,), jnp.int32),
        in_specs=[SMEM],
        out_specs=SMEM,
        name="pair_table",
    )(masks)
    heavy_rows = jnp.sum((jnp.sum(masks, axis=1) > BASE).astype(F32))
    crowded = jnp.max(copies(jnp.full((8, 128), heavy_rows), TP)) > UNITS

    gate_other, up_other, down_other = across(gate), across(up), across(down)
    rows = copies(jnp.concatenate([tokens, cotangent], axis=1), TP).reshape(-1, 2 * feat)
    rows_other, crowded = lax.optimization_barrier((across(rows), crowded))

    def partials(first_unit, with_base):
        pairs = BASE * row_blocks // 2 * with_base + EXTRA * UNITS // 2
        return pl.pallas_call(
            functools.partial(partials_kernel, t, feat, first_unit, with_base),
            out_shape=jax.ShapeDtypeStruct((pairs * ROWBLK, 3 * BLK), BF16),
            in_specs=[SMEM, SMEM] + [VMEM] * 8,
            out_specs=VMEM,
            compiler_params=PARAMS,
            name="partials",
        )(core, table, rows, rows_other, gate, gate_other, up, up_other, down, down_other)

    main = activations(partials(0, True))

    def more():
        return activations(partials(UNITS, False))

    def nothing():
        zeros = jnp.zeros((EXTRA * UNITS // 2 * ROWBLK, 3 * BLK), BF16)
        return zeros, zeros

    rest = lax.cond(crowded, more, nothing)
    acts = (*main, *rest)

    scratch = [pltpu.VMEM(((t.pairs + 1) * BLK, 3 * BLK), BF16)]
    partial_rows = pl.pallas_call(
        functools.partial(rows_kernel, t),
        out_shape=jax.ShapeDtypeStruct((row_blocks * ROWBLK, 2 * feat), BF16),
        in_specs=[SMEM, SMEM] + [ANY] * 4 + [VMEM] * 3,
        out_specs=VMEM,
        scratch_shapes=scratch + [pltpu.VMEM((row_blocks, ROWBLK, 2 * feat), F32), pltpu.SemaphoreType.DMA((4,))],
        compiler_params=PARAMS,
        name="row_grads",
    )(core, table, *acts, gate, up, down)
    out_rows = summed(partial_rows, TP).astype(BF16)

    together = 2 if blocks % 2 == 0 else 1
    columns = pl.BlockSpec((feat, together * BLK), lambda b: (0, b))
    grad_gate, grad_up, grad_down = pl.pallas_call(
        functools.partial(weights_kernel, t, together, (row_blocks * ROWBLK) ** -0.5),
        grid=(blocks // together,),
        out_shape=(
            jax.ShapeDtypeStruct(gate.shape, F32),
            jax.ShapeDtypeStruct(up.shape, F32),
            jax.ShapeDtypeStruct(down.shape, F32),
        ),
        in_specs=[SMEM, SMEM] + [ANY] * 4 + [VMEM],
        out_specs=(columns, columns, pl.BlockSpec((together * BLK, feat), lambda b: (b, 0))),
        scratch_shapes=scratch + [pltpu.VMEM((feat, row_blocks * ROWBLK), BF16), pltpu.SemaphoreType.DMA((4,))],
        compiler_params=PARAMS,
        name="weight_grads",
    )(core, table, *acts, rows)
    return out_rows[:, :feat], out_rows[:, feat:], grad_gate, grad_up, grad_down


def solution(mesh):
    fine = Mesh(mesh.devices.reshape(4, 4, 2, 2, 4), SEQ + TP)
    wide, tall = P(SEQ, TP), P(TP, SEQ)
    return jax.shard_map(
        shards,
        mesh=fine,
        in_specs=(tall, wide, wide, tall, P(None, TP), tall),
        out_specs=(tall, tall, wide, wide, tall),
        check_vma=False,
    )
```

time: 215 us -> 181 us (0.84)
  blocking collectives: 150 us -> 107 us
  starting transfers between devices: 9.91 us -> 29.6 us
  Pallas kernels: 35.6 us -> 26.5 us
  waiting for transfers between devices: 10.5 us -> 8.16 us
    all_to_all x3, blocking collectives: 75.5 us -> 53 us  [copies(): lax.all_to_all(jnp.broadcast_to(array[None], (n, *array.shape)), axis, 0,...]
    all_to_all x2, blocking collectives: 74.9 us -> 54 us  [summed(): return lax.all_to_all(tiles, axis, 0, 0, tiled=True).astype(F32).sum(axis=0)]
    pallas_call x3 -> x4, Pallas kernels: 35.6 us -> 26.5 us  [the longest x1 8.7 us: shards(): pl.pallas_call(functools.partial(weights_kernel, t, together, (row_blocks...]
    ppermute x5, waiting for transfers between devices: 10.5 us -> 1.81 us  [across(): return lax.ppermute(array, 'core', [(0, 1), (1, 0)])]
    all_to_all x1, starting transfers between devices: 4.24 us -> 12.9 us  [summed(): return lax.all_to_all(tiles, axis, 0, 0, tiled=True).astype(F32).sum(axis=0)]
    ppermute x5, starting transfers between devices: 5.67 us -> 13.4 us  [across(): return lax.ppermute(array, 'core', [(0, 1), (1, 0)])]
    all_to_all x1, waiting for transfers between devices: 0.01 us -> 6.35 us  [summed(): return lax.all_to_all(tiles, axis, 0, 0, tiled=True).astype(F32).sum(axis=0)]
    unnamed x20 -> x6, local copies, waits for them, and re-layouts: 4 us -> 0.02 us
  transfers between devices with their start and end apart: 6 -> 7, of which waited for: 3 -> 2; matrix products, arithmetic and copies ran while one was open for 0% -> 2% of each run, Pallas kernels for 7% -> 8%
where the time goes in v2:
time: 181 us
  blocking collectives  107 us (59%)
  starting transfers between devices  29.6 us (16%)
  Pallas kernels  26.5 us (15%)
  waiting for transfers between devices  8.16 us (5%)
  local copies, waits for them, and re-layouts  4.16 us (2%)
  other arithmetic  4.14 us (2%)
    all_to_all x2, blocking collectives, summed(): return lax.all_to_all(tiles, axis, 0, 0, tiled=True).astype(F32).sum(axis=0)  54 us
    all_to_all x3, blocking collectives, copies(): lax.all_to_all(jnp.broadcast_to(array[None], (n, *array.shape)), axis, 0,...  53 us
    ppermute x5, starting transfers between devices, across(): return lax.ppermute(array, 'core', [(0, 1), (1, 0)])  13.4 us
    all_to_all x1, starting transfers between devices, summed(): return lax.all_to_all(tiles, axis, 0, 0, tiled=True).astype(F32).sum(axis=0)  12.9 us
    pallas_call x1, Pallas kernels, shards(): pl.pallas_call(functools.partial(weights_kernel, t, together, (row_blocks...  8.7 us
    pallas_call x1, Pallas kernels, shards(): pl.pallas_call(functools.partial(rows_kernel, t), out_shape=jax.ShapeDtyp...  7.74 us
    all_to_all x1, waiting for transfers between devices, summed(): return lax.all_to_all(tiles, axis, 0, 0, tiled=True).astype(F32).sum(axis=0)  6.35 us
    pallas_call x1, Pallas kernels, shards(): pl.pallas_call(functools.partial(table_kernel, t), out_shape=jax.ShapeDty...  6.19 us
  transfers between devices with their start and end apart: 7, of which 2 were waited for; matrix products, arithmetic and copies ran while one was open for 2% of the time, Pallas kernels for 8%

profile of v2, /device:TPU:1, one launch (start us, length us, event | category | flops | bytes accessed | tf_op | source)
XLA Modules:
  0.0 181.1 jit_solution(12854475954760347394)
XLA Ops:
  0.6 0.0 copy-start
  0.6 0.0 copy-start.1
  0.7 0.0 copy-start.2
  0.7 1.0 pad_maximum_fusion.1
  1.7 0.1 broadcast_in_dim.17
  1.8 20.5 %all_to_all.55 = bf16[8,128,512]{2,1,0:T(8,128)(2,1)S(1)} all-to-all(bf16[8,128,512]{2,1,0:T(8,128)(2,1)S(1)} %broadcast_in_dim.17), channel_id=1, replica_groups=mesh['x'=4,'zh'=4,'core'=2,'zl'=2,'y'=4] {'zl','y'}, dimensions={0} | all-to-all | bytes 2097152 | tf_op jit(solution)/shard_map/all_to_all | solution.py:208
  22.2 2.4 %collective-permute-start.1 = (bf16[1024,512]{1,0:T(8,128)(2,1)S(1)}, bf16[1024,512]{1,0:T(8,128)(2,1)}, u32[]{:S(2)}, u32[]{:S(2)}) collective-permute-start(bf16[1024,512]{1,0:T(8,128)(2,1)S(1)} %bitcast.16), channel_id=1, source_target_pairs={{0,8},{8,0},{1,9},{9,1},{2,10},{10,2},{3,11},{11,3},{4,12},{12,4},... | collective-permute-start | bytes 3145736 | tf_op jit(solution)/shard_map/ppermute | solution.py:212
  24.7 0.0 copy-done
  24.7 0.0 collective-permute-start.2
  24.7 0.0 copy-done.1
  24.7 0.5 collective-permute-start.3
  25.2 0.1 collective-permute-start.4
  25.3 0.0 copy-done.2
  25.3 0.1 reduce_sum.66
  25.4 0.6 fusion
  26.0 1.3 broadcast_in_dim_broadcast_in_dim_broadcast_in_dim.3
  27.3 3.3 %all-to-all-start.5 = ((f32[8,8,128]{2,1,0:T(8,128)}), f32[8,8,128]{2,1,0:T(8,128)S(1)}, u32[]{:S(2)}, u32[]{:S(2)}) async-start(f32[8,8,128]{2,1,0:T(8,128)} %broadcast_in_dim_broadcast_in_dim_broadcast_in_dim.3), calls=%async_computation.5 | async-start | bytes 65536 | tf_op jit(solution)/shard_map/all_to_all | solution.py:208
  30.6 6.2 %pair_table.1.table = s32[312]{0:T(512)S(1)} custom-call(s32[8,14]{1,0:T(8,128)} %masks.1), custom_call_target="tpu_custom_call" | custom-call | tf_op jit(solution)/shard_map/pair_table/pallas_call | solution.py:244
  36.8 0.0 all-to-all-done.5
  36.8 0.6 reduce_max.9
  38.1 0.0 collective-permute-done.1.other
  38.1 0.0 collective-permute-done.2.gate_other
  38.1 0.0 collective-permute-done.3.up_other
  38.1 0.0 collective-permute-done.4.down_other
  38.1 3.9 %partials.3 = bf16[2560,384]{1,0:T(8,128)(2,1)S(1)} custom-call(s32[1]{0:T(128)} %bitcast.4.core_ref, s32[312]{0:T(512)S(1)} %pair_table.1.table, bf16[1024,512]{1,0:T(8,128)(2,1)S(1)} %bitcast.17, bf16[1024,512]{1,0:T(8,128)(2,1)} %collective-permute-done.1.other, bf16[256,1792]{1,0:T(8,128)(2,1)S(1)} %copy-done, ...), custom_call_target="tpu_custom_call" | custom-call | tf_op jit(solution)/shard_map/partials/pallas_call | solution.py:260
  42.0 27.8 %all_to_all.56 = bf16[4,640,384]{2,1,0:T(8,128)(2,1)S(1)} all-to-all(bf16[4,640,384]{2,1,0:T(8,128)(2,1)S(1)} %bitcast.14), channel_id=1, replica_groups=mesh['x'=4,'zh'=4,'core'=2,'zl'=2,'y'=4] {'x'}, dimensions={0} | all-to-all | bytes 3932160 | tf_op jit(solution)/shard_map/all_to_all | solution.py:218
  69.8 0.3 convert_reduce_fusion.1
  70.1 26.2 %all_to_all.57 = f32[4,160,384]{2,1,0:T(8,128)S(1)} all-to-all(f32[4,160,384]{2,1,0:T(8,128)S(1)} %bitcast.20), channel_id=1, replica_groups=mesh['x'=4,'zh'=4,'core'=2,'zl'=2,'y'=4] {'zh'}, dimensions={0} | all-to-all | bytes 1966080 | tf_op jit(solution)/shard_map/all_to_all | solution.py:218
  96.3 0.1 reduce_sum.69
  96.4 0.1 multiply_convert_fusion.5
  96.5 14.0 %all_to_all.58 = bf16[4,160,384]{2,1,0:T(8,128)(2,1)S(1)} all-to-all(bf16[4,160,384]{2,1,0:T(8,128)(2,1)S(1)} %broadcast_in_dim.18), channel_id=1, replica_groups=mesh['x'=4,'zh'=4,'core'=2,'zl'=2,'y'=4] {'zh'}, dimensions={0} | all-to-all | bytes 983040 | tf_op jit(solution)/shard_map/all_to_all | solution.py:208
  110.6 0.2 broadcast_in_dim.39
  110.7 18.5 %all_to_all.59 = bf16[4,640,384]{2,1,0:T(8,128)(2,1)S(1)} all-to-all(bf16[4,640,384]{2,1,0:T(8,128)(2,1)S(1)} %broadcast_in_dim.39), channel_id=1, replica_groups=mesh['x'=4,'zh'=4,'core'=2,'zl'=2,'y'=4] {'x'}, dimensions={0} | all-to-all | bytes 3932160 | tf_op jit(solution)/shard_map/all_to_all | solution.py:208
  129.2 10.3 %collective-permute-start.5 = (bf16[2560,384]{1,0:T(8,128)(2,1)S(1)}, bf16[2560,384]{1,0:T(8,128)(2,1)}, u32[]{:S(2)}, u32[]{:S(2)}) collective-permute-start(bf16[2560,384]{1,0:T(8,128)(2,1)S(1)} %bitcast.11), channel_id=1, source_target_pairs={{0,8},{8,0},{1,9},{9,1},{2,10},{10,2},{3,11},{11,3},{4,12},{12,4},... | collective-permute-start | bytes 5898248 | tf_op jit(solution)/shard_map/ppermute | solution.py:212
  139.6 1.9 %conditional.1 = (bf16[1024,384]{1,0:T(8,128)(2,1)}, bf16[1024,384]{1,0:T(8,128)(2,1)}) conditional(s32[]{:T(128)} %convert_element_type.37, () %tuple.18, (s32[1]{0:T(128)}, s32[312]{0:T(512)S(1)}, bf16[1024,512]{1,0:T(8,128)(2,1)S(1)}, bf16[1024,512]{1,0:T(8,128)(2,1)}, bf16[256,1792]{1,0:T(8,128)(2,1)}, /*index=5*/bf16[256,1792]{1,0:T(8,128)(2,1)}, ...), branch_computations={%region_5.6_spmd, %region_6.9_spmd} | conditional | flops 1040384 | bytes 10616892 | solution.py:278
  139.6 1.0 broadcast.13
  140.5 1.0 broadcast.13.clone
  141.5 1.8 collective-permute-done.5.refs_1_
  143.3 7.7 %row_grads.1 = bf16[1024,512]{1,0:T(8,128)(2,1)} custom-call(s32[1]{0:T(128)} %bitcast.4.core_ref, s32[312]{0:T(512)S(1)} %pair_table.1.table, bf16[2560,384]{1,0:T(8,128)(2,1)S(1)} %bitcast.12, bf16[2560,384]{1,0:T(8,128)(2,1)} %collective-permute-done.5.refs_1_, bf16[1024,384]{1,0:T(8,128)(2,1)} %get-tuple-element.44.refs_2_, ...), custom_call_target="tpu_custom_call" | custom-call | tf_op jit(solution)/shard_map/row_grads/pallas_call | solution.py:282
  151.1 12.9 %all-to-all-start.10 = ((bf16[8,128,512]{2,1,0:T(8,128)(2,1)}), bf16[8,128,512]{2,1,0:T(8,128)(2,1)}, u32[]{:S(2)}, u32[]{:S(2)}) async-start(bf16[8,128,512]{2,1,0:T(8,128)(2,1)} %bitcast.10), calls=%async_computation.10 | async-start | bytes 2097152 | tf_op jit(solution)/shard_map/all_to_all | solution.py:218
  164.0 8.7 %weight_grads.1 = (f32[256,1792]{1,0:T(8,128)}, f32[256,1792]{1,0:T(8,128)}, f32[1792,256]{1,0:T(8,128)}) custom-call(s32[1]{0:T(128)} %bitcast.4.core_ref, s32[312]{0:T(512)S(1)} %pair_table.1.table, bf16[2560,384]{1,0:T(8,128)(2,1)S(1)} %bitcast.13, bf16[2560,384]{1,0:T(8,128)(2,1)} %collective-permute-done.5.refs_1_, ...), custom_call_target="tpu_custom_call" | custom-call | tf_op jit(solution)/shard_map/weight_grads/pallas_call | solution.py:295
  172.7 6.3 %all-to-all-done.10 = bf16[8,128,512]{2,1,0:T(8,128)(2,1)} async-done(((bf16[8,128,512]{2,1,0:T(8,128)(2,1)}), bf16[8,128,512]{2,1,0:T(8,128)(2,1)}, u32[]{:S(2)}, u32[]{:S(2)}) %all-to-all-start.10) | async-done | bytes 1048608 | tf_op jit(solution)/shard_map/all_to_all | solution.py:218
  179.0 1.4 reduce_sum.70
  180.4 0.7 fusion.1
  (2 shorter events, 0.1 us)
Async XLA Ops:
  0.6 24.0 %copy-start = (bf16[256,1792]{1,0:T(8,128)(2,1)S(1)}, bf16[256,1792]{1,0:T(8,128)(2,1)}, u32[]{:S(2)}) copy-start(bf16[256,1792]{1,0:T(8,128)(2,1)} %refs_4_.1) | copy-start | bytes 2752516
  0.6 24.0 %copy-start.1 = (bf16[256,1792]{1,0:T(8,128)(2,1)S(1)}, bf16[256,1792]{1,0:T(8,128)(2,1)}, u32[]{:S(2)}) copy-start(bf16[256,1792]{1,0:T(8,128)(2,1)} %refs_5_.1) | copy-start | bytes 2752516
  0.7 24.6 %copy-start.2 = (s32[8,14]{1,0:T(8,128)S(1)}, s32[8,14]{1,0:T(8,128)}, u32[]{:S(2)}) copy-start(s32[8,14]{1,0:T(8,128)} %masks.1) | copy-start | bytes 1348
  22.2 15.9 %collective-permute-start.1 = (bf16[1024,512]{1,0:T(8,128)(2,1)S(1)}, bf16[1024,512]{1,0:T(8,128)(2,1)}, u32[]{:S(2)}, u32[]{:S(2)}) collective-permute-start(bf16[1024,512]{1,0:T(8,128)(2,1)S(1)} %bitcast.16), channel_id=1, source_target_pairs={{0,8},{8,0},{1,9},{9,1},{2,10},{10,2},{3,11},{11,3},{4,12},{12,4},... | collective-permute-start | bytes 3145736 | tf_op jit(solution)/shard_map/ppermute | solution.py:212
  24.7 13.4 %collective-permute-start.2 = (bf16[256,1792]{1,0:T(8,128)(2,1)S(1)}, bf16[256,1792]{1,0:T(8,128)(2,1)}, u32[]{:S(2)}, u32[]{:S(2)}) collective-permute-start(bf16[256,1792]{1,0:T(8,128)(2,1)S(1)} %copy-done), channel_id=1, source_target_pairs={{0,8},{8,0},{1,9},{9,1},{2,10},{10,2},{3,11},{11,3},{4,12},{12,4},... | collective-permute-start | bytes 2752520 | tf_op jit(solution)/shard_map/ppermute | solution.py:212
  24.7 13.4 %collective-permute-start.3 = (bf16[256,1792]{1,0:T(8,128)(2,1)S(1)}, bf16[256,1792]{1,0:T(8,128)(2,1)}, u32[]{:S(2)}, u32[]{:S(2)}) collective-permute-start(bf16[256,1792]{1,0:T(8,128)(2,1)S(1)} %copy-done.1), channel_id=1, source_target_pairs={{0,8},{8,0},{1,9},{9,1},{2,10},{10,2},{3,11},{11,3},{4,12},{12,4},... | collective-permute-start | bytes 2752520 | tf_op jit(solution)/shard_map/ppermute | solution.py:212
  25.2 12.9 %collective-permute-start.4 = (bf16[1792,256]{1,0:T(8,128)(2,1)}, bf16[1792,256]{1,0:T(8,128)(2,1)}, u32[]{:S(2)}, u32[]{:S(2)}) collective-permute-start(bf16[1792,256]{1,0:T(8,128)(2,1)} %refs_6_.1), channel_id=1, source_target_pairs={{0,8},{8,0},{1,9},{9,1},{2,10},{10,2},{3,11},{11,3},{4,12},{12,4},... | collective-permute-start | bytes 2752520 | tf_op jit(solution)/shard_map/ppermute | solution.py:212
  27.3 9.6 %all-to-all-start.5 = ((f32[8,8,128]{2,1,0:T(8,128)}), f32[8,8,128]{2,1,0:T(8,128)S(1)}, u32[]{:S(2)}, u32[]{:S(2)}) async-start(f32[8,8,128]{2,1,0:T(8,128)} %broadcast_in_dim_broadcast_in_dim_broadcast_in_dim.3), calls=%async_computation.5 | async-start | bytes 65536 | tf_op jit(solution)/shard_map/all_to_all | solution.py:208
  129.2 14.1 %collective-permute-start.5 = (bf16[2560,384]{1,0:T(8,128)(2,1)S(1)}, bf16[2560,384]{1,0:T(8,128)(2,1)}, u32[]{:S(2)}, u32[]{:S(2)}) collective-permute-start(bf16[2560,384]{1,0:T(8,128)(2,1)S(1)} %bitcast.11), channel_id=1, source_target_pairs={{0,8},{8,0},{1,9},{9,1},{2,10},{10,2},{3,11},{11,3},{4,12},{12,4},... | collective-permute-start | bytes 5898248 | tf_op jit(solution)/shard_map/ppermute | solution.py:212
  151.1 28.0 %all-to-all-start.10 = ((bf16[8,128,512]{2,1,0:T(8,128)(2,1)}), bf16[8,128,512]{2,1,0:T(8,128)(2,1)}, u32[]{:S(2)}, u32[]{:S(2)}) async-start(bf16[8,128,512]{2,1,0:T(8,128)(2,1)} %bitcast.10), calls=%async_computation.10 | async-start | bytes 2097152 | tf_op jit(solution)/shard_map/all_to_all | solution.py:218
